TPU v7x, 512 devices: a whole 4x8x8 slice. The times are simulated.
512 devices in a mesh: dp: 8 (over z), context: 16 (over y, core), tensor: 4 (over x).
Axes of the slice: x: 4, y: 8, z: 8, core: 2. Of those that a mesh axis runs over, the one named last changes fastest.
Arguments:
- layer_input: bfloat16 [8, 8192, 4096], P('dp', 'context', 'tensor'), may hold values from -6 to 6
- queries: bfloat16 [8, 16, 8192, 128], P('dp', 'tensor', 'context'), may hold values from -6 to 6
- key_states: bfloat16 [8, 4, 8192, 128], P('dp', 'tensor', 'context'), may hold values from -6 to 6
- value_states: bfloat16 [8, 4, 8192, 128], P('dp', 'tensor', 'context'), may hold values from -6 to 6
- out_grad: bfloat16 [8, 16, 8192, 128], P('dp', 'tensor', 'context'), may hold values from -0.0234375 to 0.0234375
- log_sums: bfloat16 [8, 16, 8192], P('dp', 'tensor', 'context'), may hold values from 2 to 5
- grad_dots: bfloat16 [8, 16, 8192], P('dp', 'tensor', 'context'), may hold values from -0.1875 to 0.1875
- doc_stretches: int32 [8, 10], P('dp'), may hold values from 1 to 8, as said below
- stretch_order: int32 [8, 256], P('dp'), may hold values from 0 to 255, as said below
- sign_vector: int32 [32, 128], P('context'), may hold values from -1 to 1, as said below
- exponents: int32 [8, 32], P('dp', 'context'), may hold values from 0 to 3
Outputs:
- rotated_grad: float32 [32, 128, 1024], P('context', 'dp', 'tensor')
Inputs may be any that keep to these rules, and one draw needn't show every extreme that they name: `doc_stretches`: each row gives the lengths in units of 128 tokens of 10 documents; they sum to 64. The second document is one of the longest, exactly 8 units, and begins 512 - 128 tokens after a multiple of 512 tokens. `stretch_order`: each row is a permutation of the 256 sequence blocks. Sequence blocks d * 16 to d * 16 + 15 belong to index d of context; the 16 stored blocks of one index of context hold at most 1 block belonging to any one index. `sign_vector`: every entry is 1 or -1.
All inputs are finite; a program needn't handle non-finite values.
Results may differ from a plain program's by a relative error of at most 0.0075.
Values may be sent and summed in bfloat16 or wider, within the bound.
No kernel may reach another device: no remote copies, remote signals or barrier semaphores. Data moves between devices by JAX's collectives and lax.ppermute only.
A program may use at most 64 MiB of HBM per device.

v0:
```python
import math
import jax
import jax.numpy as jnp
from jax import lax
from jax.sharding import PartitionSpec as P

HD = 128
GROUP = 4
BLK = 32
PAD = 128
HB = 128


def passed_along(block, axis, distance):
    devices = range(lax.axis_size(axis))
    route = [(i - distance, i) for i in devices if i - distance in devices]
    return lax.ppermute(block, axis, route)


def hadamard_table(table_size):
    index_row = jnp.arange(table_size, dtype=jnp.int32)
    common = jnp.bitwise_and(index_row[:, None], index_row[None, :])
    parity = jnp.zeros((table_size, table_size), jnp.int32)
    for bit_pos in range(table_size.bit_length() - 1):
        parity = parity + jnp.bitwise_and(jnp.right_shift(common, bit_pos), 1)
    signed = 1 - 2 * jnp.bitwise_and(parity, 1)
    return signed.astype(jnp.float32) * float(table_size) ** (-0.5)


def doc_of(position, ends_row):
    return jnp.sum(((position // PAD)[:, None] >= ends_row[None, :]).astype(jnp.int32), axis=1)


def live_pairs(query_pos, query_doc, key_pos, key_doc):
    return (query_doc[:, None] == key_doc[None, :]) & (key_pos[None, :] <= query_pos[:, None])


def block_grads(query_blk, grad_blk, lse_blk, dots_blk, key_blk, value_blk, live):
    scale = HD ** (-0.5)
    scores = (
        jnp.einsum("ghqd,gkd->ghqk", query_blk, key_blk, preferred_element_type=jnp.float32) * scale
    )
    probs = jnp.where(
        live[None, None], jnp.exp(scores - lse_blk.astype(jnp.float32)[..., None]), 0.0
    )
    value_part = jnp.einsum(
        "ghqk,ghqd->gkd", probs.astype(jnp.bfloat16), grad_blk, preferred_element_type=jnp.float32
    )
    dprobs = jnp.einsum("ghqd,gkd->ghqk", grad_blk, value_blk, preferred_element_type=jnp.float32)
    dscores = (probs * (dprobs - dots_blk.astype(jnp.float32)[..., None])).astype(jnp.bfloat16)
    key_part = (
        jnp.einsum("ghqk,ghqd->gkd", dscores, query_blk, preferred_element_type=jnp.float32) * scale
    )
    return (key_part, value_part)


def per_device(
    layer_input,
    queries,
    key_states,
    value_states,
    out_grad,
    log_sums,
    grad_dots,
    doc_stretches,
    stretch_order,
    sign_vector,
    exponents,
):
    local_tokens = queries.shape[2]
    local_kv = key_states.shape[1]
    local_cols = 2 * local_kv * HD
    order_row = stretch_order[0]
    ends_row = jnp.cumsum(doc_stretches[0])
    groups = lax.axis_size("context")
    slot_count = local_tokens // BLK
    capacity = max(1, slot_count // groups)
    device_id = lax.axis_index("context")
    order_grid = order_row.reshape(groups, slot_count)
    own_order = lax.dynamic_slice_in_dim(order_row, device_id * slot_count, slot_count, 0)
    own_target = own_order // slot_count
    slot_ids = jnp.arange(slot_count, dtype=jnp.int32)
    earlier = slot_ids[None, :] < slot_ids[:, None]
    send_rank = jnp.sum(
        jnp.where(earlier & (own_target[None, :] == own_target[:, None]), 1, 0), axis=1
    )
    send_row = own_target * capacity + send_rank
    buffer_ids = jnp.arange(groups * capacity, dtype=jnp.int32)
    send_table = (buffer_ids[:, None] == send_row[None, :]).astype(jnp.bfloat16)
    wanted = device_id * slot_count + slot_ids
    stretch_ids = jnp.arange(order_row.shape[0], dtype=jnp.int32)
    stored_at = jnp.sum(
        jnp.where(order_row[None, :] == wanted[:, None], stretch_ids[None, :], 0), axis=1
    )
    source = stored_at // slot_count
    source_slot = stored_at % slot_count
    source_orders = jnp.take(order_grid, source, axis=0)
    same_target = source_orders // slot_count == device_id
    recv_rank = jnp.sum(
        jnp.where(same_target & (slot_ids[None, :] < source_slot[:, None]), 1, 0), axis=1
    )
    recv_row = source * capacity + recv_rank
    recv_table = (recv_row[:, None] == buffer_ids[None, :]).astype(jnp.bfloat16)

    def pack(array):
        blocks = array[0].reshape(array.shape[1], slot_count, -1)
        return jnp.einsum(
            "rt,htx->rhx", send_table, blocks, preferred_element_type=jnp.float32
        ).astype(jnp.bfloat16)

    def unpack(packed):
        placed = jnp.einsum(
            "sr,rhx->hsx", recv_table, packed, preferred_element_type=jnp.float32
        ).astype(jnp.bfloat16)
        return placed.reshape(packed.shape[1], local_tokens, -1)

    moved = (
        lax.all_to_all(pack(queries), "context", split_axis=0, concat_axis=0, tiled=True),
        lax.all_to_all(pack(out_grad), "context", split_axis=0, concat_axis=0, tiled=True),
        lax.all_to_all(pack(key_states), "context", split_axis=0, concat_axis=0, tiled=True),
        lax.all_to_all(pack(value_states), "context", split_axis=0, concat_axis=0, tiled=True),
        lax.all_to_all(pack(log_sums), "context", split_axis=0, concat_axis=0, tiled=True),
        lax.all_to_all(pack(grad_dots), "context", split_axis=0, concat_axis=0, tiled=True),
    )
    query_sorted = unpack(moved[0])
    grad_sorted = unpack(moved[1])
    key_sorted = unpack(moved[2])
    value_sorted = unpack(moved[3])
    lse_sorted = unpack(moved[4])[:, :, 0]
    dots_sorted = unpack(moved[5])[:, :, 0]
    total_len = local_tokens * groups
    longest_tokens = max(total_len // PAD // 8, local_tokens // PAD) * PAD
    reach = (local_tokens - PAD + longest_tokens - 1) // local_tokens
    query_list = [query_sorted]
    grad_list = [grad_sorted]
    lse_list = [lse_sorted]
    dots_list = [dots_sorted]
    for ahead in range(1, reach + 1):
        later = passed_along(
            (query_sorted, grad_sorted, lse_sorted, dots_sorted), "context", -ahead
        )
        query_list.append(later[0])
        grad_list.append(later[1])
        lse_list.append(later[2])
        dots_list.append(later[3])
    all_query = jnp.concatenate(query_list, axis=1)
    all_grad = jnp.concatenate(grad_list, axis=1)
    all_lse = jnp.concatenate(lse_list, axis=1)
    all_dots = jnp.concatenate(dots_list, axis=1)
    total_rows = all_query.shape[1]
    query_pos_all = device_id * local_tokens + jnp.arange(total_rows, dtype=jnp.int32)
    query_doc_all = doc_of(query_pos_all, ends_row)
    key_pos_own = device_id * local_tokens + jnp.arange(local_tokens, dtype=jnp.int32)
    key_doc_own = doc_of(key_pos_own, ends_row)
    step_len = math.gcd(total_rows, 640)

    def ahead_block(index_val, running):
        offset = index_val * step_len
        query_blk = lax.dynamic_slice_in_dim(all_query, offset, step_len, 1).reshape(
            local_kv, GROUP, step_len, HD
        )
        grad_blk = lax.dynamic_slice_in_dim(all_grad, offset, step_len, 1).reshape(
            local_kv, GROUP, step_len, HD
        )
        lse_blk = lax.dynamic_slice_in_dim(all_lse, offset, step_len, 1).reshape(
            local_kv, GROUP, step_len
        )
        dots_blk = lax.dynamic_slice_in_dim(all_dots, offset, step_len, 1).reshape(
            local_kv, GROUP, step_len
        )
        query_pos = lax.dynamic_slice_in_dim(query_pos_all, offset, step_len, 0)
        query_doc = lax.dynamic_slice_in_dim(query_doc_all, offset, step_len, 0)
        live = live_pairs(query_pos, query_doc, key_pos_own, key_doc_own)
        key_part, value_part = block_grads(
            query_blk, grad_blk, lse_blk, dots_blk, key_sorted, value_sorted, live
        )
        return (running[0] + key_part, running[1] + value_part)

    empty = jnp.zeros((local_kv, local_tokens, HD), jnp.float32)
    key_total, value_total = lax.fori_loop(0, total_rows // step_len, ahead_block, (empty, empty))
    stacked = jnp.stack([key_total, value_total], axis=1)
    sorted_rows = (
        jnp.transpose(stacked, (2, 0, 1, 3))
        .reshape(slot_count, BLK * local_cols)
        .astype(jnp.bfloat16)
    )
    outgoing = jnp.einsum(
        "sr,sx->rx", recv_table, sorted_rows, preferred_element_type=jnp.float32
    ).astype(jnp.bfloat16)
    returned = lax.all_to_all(outgoing, "context", split_axis=0, concat_axis=0, tiled=True)
    stored_rows = jnp.einsum(
        "rt,rx->tx", send_table, returned, preferred_element_type=jnp.float32
    ).astype(jnp.bfloat16)
    kv_local = stored_rows.reshape(local_tokens, local_cols)[None]
    full_input = lax.all_gather(layer_input, "tensor", axis=2, tiled=True)
    row_input = lax.all_to_all(full_input, "context", split_axis=2, concat_axis=1, tiled=True)
    span = row_input[0]
    member_grad = jnp.einsum(
        "td,tc->dc",
        span,
        lax.all_gather(kv_local, "context", axis=1, tiled=True)[0],
        preferred_element_type=jnp.float32,
    )
    local_blocks = sign_vector.shape[0]
    had = hadamard_table(HB)
    shaped = (
        member_grad.reshape(local_blocks, HB, local_cols)
        * sign_vector.astype(jnp.float32)[:, :, None]
    )
    rotated = jnp.einsum("ij,bjc->bic", had, shaped, precision=lax.Precision.HIGHEST)
    factor = 1.0 / jnp.left_shift(jnp.int32(1), exponents[0]).astype(jnp.float32)
    quantized = (rotated * factor[:, None, None]).astype(jnp.bfloat16)
    spread = lax.all_to_all(quantized[None], "dp", split_axis=2, concat_axis=0, tiled=True)
    return jnp.sum(spread.astype(jnp.float32), axis=0)


def solution(mesh):
    return jax.shard_map(
        per_device,
        mesh=mesh,
        in_specs=(
            P("dp", "context", "tensor"),
            P("dp", "tensor", "context", None),
            P("dp", "tensor", "context", None),
            P("dp", "tensor", "context", None),
            P("dp", "tensor", "context", None),
            P("dp", "tensor", "context"),
            P("dp", "tensor", "context"),
            P("dp", None),
            P("dp", None),
            P("context", None),
            P("dp", "context"),
        ),
        out_specs=P("context", "dp", "tensor"),
        check_vma=False,
    )
```

profile of v0, /device:TPU:6, one launch (start us, length us, event | category | flops | bytes accessed | tf_op | source)
XLA Modules:
  0.0 429.9 jit_solution(6349806971333252527)
XLA Ops:
  12.0 7.2 %all-to-all-start.2 = ((bf16[16,4,32]{2,1,0:T(4,128)(2,1)}), bf16[16,4,32]{2,1,0:T(4,128)(2,1)S(1)}, u32[]{:S(2)}, u32[]{:S(2)}) async-start(bf16[16,4,32]{2,1,0:T(4,128)(2,1)} %copy.89), calls=%async_computation.2 | async-start | bytes 32768 | tf_op jit(solution)/shard_map/all_to_all | solution.py:122
  22.9 4.0 all-to-all-done.2
  26.9 3.5 all-to-all-start.5
  38.2 7.1 %all-to-all-start = ((bf16[16,4,4096]{2,1,0:T(4,128)(2,1)}), bf16[16,4,4096]{2,1,0:T(4,128)(2,1)S(1)}, u32[]{:S(2)}, u32[]{:S(2)}) async-start(bf16[16,4,4096]{2,1,0:T(4,128)(2,1)} %copy.86), calls=%async_computation | async-start | bytes 1048576 | tf_op jit(solution)/shard_map/all_to_all | solution.py:118
  45.8 15.6 %all-to-all-done = bf16[16,4,4096]{2,1,0:T(4,128)(2,1)S(1)} async-done(((bf16[16,4,4096]{2,1,0:T(4,128)(2,1)}), bf16[16,4,4096]{2,1,0:T(4,128)(2,1)S(1)}, u32[]{:S(2)}, u32[]{:S(2)}) %all-to-all-start) | async-done | bytes 524320 | tf_op jit(solution)/shard_map/all_to_all | solution.py:118
  61.3 4.2 all-to-all-start.3
  71.3 8.8 %collective-permute-done.3 = bf16[4,512]{1,0:T(4,128)(2,1)S(1)} collective-permute-done((bf16[4,512]{1,0:T(4,128)(2,1)S(1)}, bf16[4,512]{1,0:T(4,128)(2,1)S(1)}, u32[]{:S(2)}, u32[]{:S(2)}) %collective-permute-start.3) | collective-permute-done | bytes 4128 | tf_op jit(solution)/shard_map/ppermute | solution.py:17
  83.4 9.8 %all-to-all-start.1 = ((bf16[16,2,2048]{2,1,0:T(2,128)(2,1)}), bf16[16,2,2048]{2,1,0:T(2,128)(2,1)S(1)}, u32[]{:S(2)}, u32[]{:S(2)}) async-start(bf16[16,2,2048]{2,1,0:T(2,128)(2,1)} %reshape.396), calls=%async_computation.1 | async-start | bytes 262144 | tf_op jit(solution)/shard_map/all_to_all | solution.py:120
  95.2 16.5 %all-to-all-done.1 = bf16[16,2,2048]{2,1,0:T(2,128)(2,1)S(1)} async-done(((bf16[16,2,2048]{2,1,0:T(2,128)(2,1)}), bf16[16,2,2048]{2,1,0:T(2,128)(2,1)S(1)}, u32[]{:S(2)}, u32[]{:S(2)}) %all-to-all-start.1) | async-done | bytes 131104 | tf_op jit(solution)/shard_map/all_to_all | solution.py:120
  111.8 5.7 %all-to-all-start.4 = ((bf16[16,2,2048]{2,1,0:T(2,128)(2,1)}), bf16[16,2,2048]{2,1,0:T(2,128)(2,1)S(1)}, u32[]{:S(2)}, u32[]{:S(2)}) async-start(bf16[16,2,2048]{2,1,0:T(2,128)(2,1)} %reshape.398), calls=%async_computation.4 | async-start | bytes 262144 | tf_op jit(solution)/shard_map/all_to_all | solution.py:121
  119.3 6.9 %all-to-all-done.4 = bf16[16,2,2048]{2,1,0:T(2,128)(2,1)S(1)} async-done(((bf16[16,2,2048]{2,1,0:T(2,128)(2,1)}), bf16[16,2,2048]{2,1,0:T(2,128)(2,1)S(1)}, u32[]{:S(2)}, u32[]{:S(2)}) %all-to-all-start.4) | async-done | bytes 131104 | tf_op jit(solution)/shard_map/all_to_all | solution.py:121
  126.7 2.3 pad_maximum_fusion
  129.0 1.3 pad_maximum_fusion.1
  130.3 44.5 %while.16 = (s32[]{:T(128)}, f32[1,512,128]{2,1,0:T(8,128)S(1)}, f32[1,512,128]{2,1,0:T(8,128)S(1)}, s32[1536]{0:T(1024)S(1)}, s32[512]{0:T(512)S(1)}, /*index=5...) while((s32[]{:T(128)}, f32[1,512,128]{2,1,0:T(8,128)S(1)}, ...), condition=%wide.region_7.8_spmd.clone, body=%wide.region_6.7_spmd.clone.sunk | while | flops 270796288 | bytes 5133045 | solution.py:180
  130.7 1.3 fusion.160
  132.0 1.7 fusion.161
  134.4 1.3 fusion.160
  135.7 1.7 fusion.161
  138.1 1.3 fusion.160
  139.4 1.7 fusion.161
  141.8 1.3 fusion.160
  143.1 1.7 fusion.161
  145.5 1.3 fusion.160
  146.8 1.7 fusion.161
  149.2 1.3 fusion.160
  150.5 1.7 fusion.161
  152.9 1.3 fusion.160
  154.2 1.7 fusion.161
  156.6 1.3 fusion.160
  157.9 1.7 fusion.161
  160.3 1.3 fusion.160
  161.7 1.7 fusion.161
  165.4 1.7 fusion.161
  167.8 1.3 fusion.160
  169.1 1.7 fusion.161
  171.5 1.3 fusion.160
  172.8 1.7 fusion.161
  176.7 17.0 %all_to_all.66 = bf16[16,2,4096]{2,1,0:T(2,128)(2,1)S(1)} all-to-all(bf16[16,2,4096]{2,1,0:T(2,128)(2,1)S(1)} %reshape.400), channel_id=1, replica_groups=mesh['dp'=8,'context'=16,'tensor'=4] {'context'}, dimensions={0} | all-to-all | bytes 524288 | tf_op jit(solution)/shard_map/all_to_all | solution.py:190
  194.0 18.9 %copy.98 = bf16[1,512,4096]{1,0,2:T(2,128)(2,1)} copy(bf16[1,512,4096]{2,1,0:T(8,128)(2,1)} %all-gather.5.cloned.1.call-done) | data formatting | bytes 8388608 | tf_op jit(solution)/shard_map/all_gather | solution.py:195
  212.9 28.5 %reduce.7 = bf16[4096,512]{1,0:T(8,128)(2,1)} reduce(bf16[4096,1,512]{2,1,0:T(2,128)(2,1)} %bitcast.157, bf16[]{:T(256)} %broadcast.474), dimensions={1}, to_apply=%bitcast.136.reduce_sub_computation | reduce | bytes 8388610
  241.4 11.4 %reshape.394 = bf16[16,2,65536]{2,1,0:T(2,128)(2,1)} reshape(bf16[4096,512]{1,0:T(8,128)(2,1)} %reduce.7) | data formatting | bytes 8388608
  252.8 4.7 %all-to-all-start.7 = ((bf16[16,2,65536]{2,1,0:T(2,128)(2,1)}), bf16[16,2,65536]{2,1,0:T(2,128)(2,1)}, u32[]{:S(2)}, u32[]{:S(2)}) async-start(bf16[16,2,65536]{2,1,0:T(2,128)(2,1)} %reshape.394), calls=%async_computation.7 | async-start | bytes 8388608 | tf_op jit(solution)/shard_map/all_to_all | solution.py:196
  258.9 112.6 %all-to-all-done.7 = bf16[16,2,65536]{2,1,0:T(2,128)(2,1)} async-done(((bf16[16,2,65536]{2,1,0:T(2,128)(2,1)}), bf16[16,2,65536]{2,1,0:T(2,128)(2,1)}, u32[]{:S(2)}, u32[]{:S(2)}) %all-to-all-start.7) | async-done | bytes 4194336 | tf_op jit(solution)/shard_map/all_to_all | solution.py:196
  371.4 12.3 %reshape.395 = bf16[4096,1,512]{2,1,0:T(2,128)(2,1)} reshape(bf16[16,2,65536]{2,1,0:T(2,128)(2,1)} %all-to-all-done.7) | data formatting | bytes 8388608
  383.8 6.5 %copy.108 = bf16[1,512,4096]{1,2,0:T(8,128)(2,1)} copy(bf16[1,512,4096]{1,0,2:T(2,128)(2,1)} %bitcast.158) | data formatting | bytes 8388608
  390.3 6.4 %copy.99 = bf16[1,16,512,256]{3,2,1,0:T(8,128)(2,1)} copy(bf16[1,16,512,256]{2,3,1,0:T(8,128)(2,1)} %bitcast.159) | data formatting | bytes 8388608 | tf_op jit(solution)/shard_map/all_to_all | solution.py:196
  396.7 5.2 %fusion.34 = f32[256,256]{0,1:T(8,128)S(1)} fusion(bf16[8192,256]{1,0:T(8,128)(2,1)} %bitcast.160, bf16[1,8192,256]{2,1,0:T(8,128)(2,1)} %all-gather.3.cloned.1.call-done), kind=kOutput, calls=%fused_computation.48 | convolution fusion | flops 1073741824 | bytes 8650752 | tf_op jit(solution)/shard_map/td,tc->dc/dot_general | solution.py:198
  402.6 19.2 %all_to_all.67 = bf16[1,2,128,256]{3,1,0,2:T(2,128)(2,1)S(1)} all-to-all(bf16[1,2,128,256]{3,1,0,2:T(2,128)(2,1)S(1)} %copy.101), channel_id=1, replica_groups=mesh['dp'=8,'context'=16,'tensor'=4] {'dp'}, dimensions={2} | all-to-all | bytes 262144 | tf_op jit(solution)/shard_map/all_to_all | solution.py:213
  (190 shorter events, 43.7 us)
Async XLA Ops:
  7.4 13.5 %copy-start.3 = (s32[1,256]{1,0:T(1,128)S(1)}, s32[1,256]{1,0:T(1,128)}, u32[]{:S(2)}) copy-start(s32[1,256]{1,0:T(1,128)} %param.21) | copy-start | bytes 3076
  7.4 13.7 %copy-start.1 = (bf16[1,1,512,128]{3,2,1,0:T(8,128)(2,1)S(1)}, bf16[1,1,512,128]{3,2,1,0:T(8,128)(2,1)}, u32[]{:S(2)}) copy-start(bf16[1,1,512,128]{3,2,1,0:T(8,128)(2,1)} %param.15) | copy-start | bytes 393220
  7.4 13.9 %copy-start = (bf16[1,4,512,128]{3,2,1,0:T(8,128)(2,1)S(1)}, bf16[1,4,512,128]{3,2,1,0:T(8,128)(2,1)}, u32[]{:S(2)}) copy-start(bf16[1,4,512,128]{3,2,1,0:T(8,128)(2,1)} %param.17) | copy-start | bytes 1572868
  7.4 14.4 %copy-start.2 = (bf16[1,1,512,128]{3,2,1,0:T(8,128)(2,1)S(1)}, bf16[1,1,512,128]{3,2,1,0:T(8,128)(2,1)}, u32[]{:S(2)}) copy-start(bf16[1,1,512,128]{3,2,1,0:T(8,128)(2,1)} %param.16) | copy-start | bytes 393220
  7.4 14.5 %copy-start.4 = (bf16[1,4,512]{2,1,0:T(4,128)(2,1)S(1)}, bf16[1,4,512]{2,1,0:T(4,128)(2,1)}, u32[]{:S(2)}) copy-start(bf16[1,4,512]{2,1,0:T(4,128)(2,1)} %param.19) | copy-start | bytes 12292
  7.4 23.0 %copy-start.6 = (s32[1,10]{1,0:T(1,128)S(1)}, s32[1,10]{1,0:T(1,128)}, u32[]{:S(2)}) copy-start(s32[1,10]{1,0:T(1,128)} %param.20) | copy-start | bytes 124
  7.4 186.6 %all-gather.5.cloned.1.call-start = ((), (), s32[]{:S(2)}) async-start(), calls=%async_computation.10 | async-start | bytes 5242880 | tf_op jit(solution)/shard_map/all_gather | solution.py:195
  12.0 14.8 %all-to-all-start.2 = ((bf16[16,4,32]{2,1,0:T(4,128)(2,1)}), bf16[16,4,32]{2,1,0:T(4,128)(2,1)S(1)}, u32[]{:S(2)}, u32[]{:S(2)}) async-start(bf16[16,4,32]{2,1,0:T(4,128)(2,1)} %copy.89), calls=%async_computation.2 | async-start | bytes 32768 | tf_op jit(solution)/shard_map/all_to_all | solution.py:122
  26.9 11.3 %all-to-all-start.5 = ((bf16[16,4,32]{2,1,0:T(4,128)(2,1)}), bf16[16,4,32]{2,1,0:T(4,128)(2,1)S(1)}, u32[]{:S(2)}, u32[]{:S(2)}) async-start(bf16[16,4,32]{2,1,0:T(4,128)(2,1)} %copy.94), calls=%async_computation.5 | async-start | bytes 32768 | tf_op jit(solution)/shard_map/all_to_all | solution.py:123
  38.2 23.2 %all-to-all-start = ((bf16[16,4,4096]{2,1,0:T(4,128)(2,1)}), bf16[16,4,4096]{2,1,0:T(4,128)(2,1)S(1)}, u32[]{:S(2)}, u32[]{:S(2)}) async-start(bf16[16,4,4096]{2,1,0:T(4,128)(2,1)} %copy.86), calls=%async_computation | async-start | bytes 1048576 | tf_op jit(solution)/shard_map/all_to_all | solution.py:118
  61.3 22.0 %all-to-all-start.3 = ((bf16[16,4,4096]{2,1,0:T(4,128)(2,1)}), bf16[16,4,4096]{2,1,0:T(4,128)(2,1)S(1)}, u32[]{:S(2)}, u32[]{:S(2)}) async-start(bf16[16,4,4096]{2,1,0:T(4,128)(2,1)} %copy.91), calls=%async_computation.3 | async-start | bytes 1048576 | tf_op jit(solution)/shard_map/all_to_all | solution.py:119
  65.8 14.2 %collective-permute-start.3 = (bf16[4,512]{1,0:T(4,128)(2,1)S(1)}, bf16[4,512]{1,0:T(4,128)(2,1)S(1)}, u32[]{:S(2)}, u32[]{:S(2)}) collective-permute-start(bf16[4,512]{1,0:T(4,128)(2,1)S(1)} %squeeze_reshape.6), channel_id=1, source_target_pairs={{8,0},{12,4},{16,8},{20,12},{24,16},{28,20},{32,24},{36,28},{40,32... | collective-permute-start | bytes 12296 | tf_op jit(solution)/shard_map/ppermute | solution.py:17
  67.1 13.0 %collective-permute-start.2 = (bf16[4,512]{1,0:T(4,128)(2,1)S(1)}, bf16[4,512]{1,0:T(4,128)(2,1)S(1)}, u32[]{:S(2)}, u32[]{:S(2)}) collective-permute-start(bf16[4,512]{1,0:T(4,128)(2,1)S(1)} %squeeze_reshape.6), channel_id=1, source_target_pairs={{4,0},{8,4},{12,8},{16,12},{20,16},{24,20},{28,24},{32,28},{36,32}... | collective-permute-start | bytes 12296 | tf_op jit(solution)/shard_map/ppermute | solution.py:17
  68.7 48.7 %collective-permute-start.7 = (bf16[4,512]{1,0:T(4,128)(2,1)S(1)}, bf16[4,512]{1,0:T(4,128)(2,1)S(1)}, u32[]{:S(2)}, u32[]{:S(2)}) collective-permute-start(bf16[4,512]{1,0:T(4,128)(2,1)S(1)} %squeeze_reshape.7), channel_id=1, source_target_pairs={{8,0},{12,4},{16,8},{20,12},{24,16},{28,20},{32,24},{36,28},{40,32... | collective-permute-start | bytes 12296 | tf_op jit(solution)/shard_map/ppermute | solution.py:17
  70.0 48.8 %collective-permute-start.6 = (bf16[4,512]{1,0:T(4,128)(2,1)S(1)}, bf16[4,512]{1,0:T(4,128)(2,1)S(1)}, u32[]{:S(2)}, u32[]{:S(2)}) collective-permute-start(bf16[4,512]{1,0:T(4,128)(2,1)S(1)} %squeeze_reshape.7), channel_id=1, source_target_pairs={{4,0},{8,4},{12,8},{16,12},{20,16},{24,20},{28,24},{32,28},{36,32}... | collective-permute-start | bytes 12296 | tf_op jit(solution)/shard_map/ppermute | solution.py:17
  80.8 45.9 %collective-permute-start.1 = (bf16[4,512,128]{2,1,0:T(8,128)(2,1)S(1)}, bf16[4,512,128]{2,1,0:T(8,128)(2,1)S(1)}, u32[]{:S(2)}, u32[]{:S(2)}) collective-permute-start(bf16[4,512,128]{2,1,0:T(8,128)(2,1)S(1)} %reshape.358), channel_id=1, source_target_pairs={{8,0},{12,4},{16,8},{20,12},{24,16},{28,20},{32,24},{36,28},{40,32... | collective-permute-start | bytes 1572872 | tf_op jit(solution)/shard_map/ppermute | solution.py:17
  82.1 44.6 %collective-permute-start = (bf16[4,512,128]{2,1,0:T(8,128)(2,1)S(1)}, bf16[4,512,128]{2,1,0:T(8,128)(2,1)}, u32[]{:S(2)}, u32[]{:S(2)}) collective-permute-start(bf16[4,512,128]{2,1,0:T(8,128)(2,1)S(1)} %reshape.358), channel_id=1, source_target_pairs={{4,0},{8,4},{12,8},{16,12},{20,16},{24,20},{28,24},{32,28},{36,32}... | collective-permute-start | bytes 1572872 | tf_op jit(solution)/shard_map/ppermute | solution.py:17
  83.4 28.4 %all-to-all-start.1 = ((bf16[16,2,2048]{2,1,0:T(2,128)(2,1)}), bf16[16,2,2048]{2,1,0:T(2,128)(2,1)S(1)}, u32[]{:S(2)}, u32[]{:S(2)}) async-start(bf16[16,2,2048]{2,1,0:T(2,128)(2,1)} %reshape.396), calls=%async_computation.1 | async-start | bytes 262144 | tf_op jit(solution)/shard_map/all_to_all | solution.py:120
  93.9 35.1 %collective-permute-start.5 = (bf16[4,512,128]{2,1,0:T(8,128)(2,1)S(1)}, bf16[4,512,128]{2,1,0:T(8,128)(2,1)}, u32[]{:S(2)}, u32[]{:S(2)}) collective-permute-start(bf16[4,512,128]{2,1,0:T(8,128)(2,1)S(1)} %reshape.362), channel_id=1, source_target_pairs={{8,0},{12,4},{16,8},{20,12},{24,16},{28,20},{32,24},{36,28},{40,32... | collective-permute-start | bytes 1572872 | tf_op jit(solution)/shard_map/ppermute | solution.py:17
  111.8 14.4 %all-to-all-start.4 = ((bf16[16,2,2048]{2,1,0:T(2,128)(2,1)}), bf16[16,2,2048]{2,1,0:T(2,128)(2,1)S(1)}, u32[]{:S(2)}, u32[]{:S(2)}) async-start(bf16[16,2,2048]{2,1,0:T(2,128)(2,1)} %reshape.398), calls=%async_computation.4 | async-start | bytes 262144 | tf_op jit(solution)/shard_map/all_to_all | solution.py:121
  117.5 11.6 %collective-permute-start.4 = (bf16[4,512,128]{2,1,0:T(8,128)(2,1)S(1)}, bf16[4,512,128]{2,1,0:T(8,128)(2,1)}, u32[]{:S(2)}, u32[]{:S(2)}) collective-permute-start(bf16[4,512,128]{2,1,0:T(8,128)(2,1)S(1)} %reshape.362), channel_id=1, source_target_pairs={{4,0},{8,4},{12,8},{16,12},{20,16},{24,20},{28,24},{32,28},{36,32}... | collective-permute-start | bytes 1572872 | tf_op jit(solution)/shard_map/ppermute | solution.py:17
  252.8 6.0 %copy-start.5 = (s32[2,128]{1,0:T(2,128)S(1)}, s32[2,128]{1,0:T(2,128)}, u32[]{:S(2)}) copy-start(s32[2,128]{1,0:T(2,128)} %param.22) | copy-start | bytes 3076
  252.8 6.0 %copy-start.7 = (s32[1,2]{1,0:T(1,128)S(1)}, s32[1,2]{1,0:T(1,128)}, u32[]{:S(2)}) copy-start(s32[1,2]{1,0:T(1,128)} %param.23) | copy-start | bytes 28
  252.8 118.6 %all-to-all-start.7 = ((bf16[16,2,65536]{2,1,0:T(2,128)(2,1)}), bf16[16,2,65536]{2,1,0:T(2,128)(2,1)}, u32[]{:S(2)}, u32[]{:S(2)}) async-start(bf16[16,2,65536]{2,1,0:T(2,128)(2,1)} %reshape.394), calls=%async_computation.7 | async-start | bytes 8388608 | tf_op jit(solution)/shard_map/all_to_all | solution.py:196
  257.5 139.2 %all-gather.3.cloned.1.call-start = ((), (), s32[]{:S(2)}) async-start(), calls=%async_computation.9 | async-start | bytes 4456448 | tf_op jit(solution)/shard_map/all_gather | solution.py:201
Sparse Core Ops, SparseCore 0:
  10.3 56.3 all-gather.4
Sparse Core Ops, SparseCore 1:
  260.1 110.8 all-gather.2
where the time goes:
time: 433 us; the launch traced here: 430 us
  waiting for transfers between devices  165 us (38%)
  local copies, waits for them, and re-layouts  69.7 us (16%)
  starting transfers between devices  52.6 us (12%)
  matrix products  49.4 us (11%)
  other arithmetic  40.5 us (9%)
  blocking collectives  36.2 us (8%)
  between operations  15.5 us (4%)
    all_to_all x1, waiting for transfers between devices, per_device(): lax.all_to_all(full_input, 'context', split_axis=2, concat_axis=1, tiled=...  113 us
    unnamed x27, local copies, waits for them, and re-layouts  33.5 us
    unnamed x4, other arithmetic  29.1 us
    dot_general x12, matrix products, block_grads(): jnp.einsum('ghqk,ghqd->gkd', dscores, query_blk, preferred_element_type=j...  19.9 us
    all_to_all x1, blocking collectives, per_device(): lax.all_to_all(quantized[None], 'dp', split_axis=2, concat_axis=0, tiled=...  19.2 us
    all_gather x1, local copies, waits for them, and re-layouts, per_device(): full_input = lax.all_gather(layer_input, 'tensor', axis=2, tiled=True)  18.9 us
    all_to_all x1, blocking collectives, per_device(): lax.all_to_all(outgoing, 'context', split_axis=0, concat_axis=0, tiled=True)  17 us
    all_to_all x1, waiting for transfers between devices, per_device(): lax.all_to_all(pack(key_states), 'context', split_axis=0, concat_axis=0,...  16.5 us
  transfers between devices with their start and end apart: 17, of which 6 were waited for; matrix products, arithmetic and copies ran while one was open for 22% of the time, Pallas kernels for 0%

commit v1 on v0

--- a/solution.py
+++ b/solution.py
@@ -192,7 +192,23 @@
         "rt,rx->tx", send_table, returned, preferred_element_type=jnp.float32
     ).astype(jnp.bfloat16)
     kv_local = stored_rows.reshape(local_tokens, local_cols)[None]
-    full_input = lax.all_gather(layer_input, "tensor", axis=2, tiled=True)
+    ways, here, hop = (lax.axis_size("tensor"), lax.axis_index("tensor"), layer_input.shape[2])
+    lengths = [n * ways if d == 2 else n for d, n in enumerate(layer_input.shape)]
+    full = lax.dynamic_update_slice_in_dim(
+        jnp.zeros(lengths, layer_input.dtype), layer_input, here * hop, axis=2
+    )
+    going_up = going_down = layer_input
+    for far in range(1, ways // 2 + 1):
+        going_up = lax.ppermute(going_up, "tensor", [(d, (d + 1) % ways) for d in range(ways)])
+        full = lax.dynamic_update_slice_in_dim(full, going_up, (here - far) % ways * hop, axis=2)
+        if 2 * far < ways:
+            going_down = lax.ppermute(
+                going_down, "tensor", [(d, (d - 1) % ways) for d in range(ways)]
+            )
+            full = lax.dynamic_update_slice_in_dim(
+                full, going_down, (here + far) % ways * hop, axis=2
+            )
+    full_input = full
     row_input = lax.all_to_all(full_input, "context", split_axis=2, concat_axis=1, tiled=True)
     span = row_input[0]
     member_grad = jnp.einsum(

time: 433 us -> 439 us (1.014)
  local copies, waits for them, and re-layouts: 69.7 us -> 98.8 us
  blocking collectives: 36.2 us -> 17.6 us
  waiting for transfers between devices: 165 us -> 147 us
  starting transfers between devices: 52.6 us -> 67.8 us
    all_gather x1 -> x0, local copies, waits for them, and re-layouts: 18.9 us -> none  [per_device(): full_input = lax.all_gather(layer_input, 'tensor', axis=2, tiled=True)]
    all_to_all x1 -> x0, blocking collectives: 17 us -> none  [per_device(): lax.all_to_all(outgoing, 'context', split_axis=0, concat_axis=0, tiled=True)]
    ppermute x0 -> x3, local copies, waits for them, and re-layouts: none -> 16.6 us  [the longest x2 10.6 us: per_device(): lax.ppermute(going_up, 'tensor', [(d, (d + 1) % ways) for d in range(ways)])]
    ppermute x0 -> x3, starting transfers between devices: none -> 15.1 us  [the longest x2 13.2 us: per_device(): lax.ppermute(going_up, 'tensor', [(d, (d + 1) % ways) for d in range(ways)])]
    dynamic_update_slice x0 -> x4, local copies, waits for them, and re-layouts: none -> 14 us  [the longest x2 6.96 us: per_device(): lax.dynamic_update_slice_in_dim(full, going_up, (here - far) % ways * hop...]
    all_to_all x1, waiting for transfers between devices: 16.5 us -> 6.75 us  [per_device(): lax.all_to_all(pack(key_states), 'context', split_axis=0, concat_axis=0,...]
    all_to_all x1, waiting for transfers between devices: 15.6 us -> 6.04 us  [per_device(): lax.all_to_all(pack(queries), 'context', split_axis=0, concat_axis=0, til...]
    dot_general x0 -> x1, local copies, waits for them, and re-layouts: none -> 6.33 us  [per_device(): jnp.einsum('td,tc->dc', span, lax.all_gather(kv_local, 'context', axis=1,...]
  transfers between devices with their start and end apart: 17 -> 20, of which waited for: 6 -> 7; matrix products, arithmetic and copies ran while one was open for 22% -> 31% of each run, Pallas kernels for 0% -> 0%
where the time goes in v1:
time: 439 us; the launch traced here: 436 us
  waiting for transfers between devices  147 us (33%)
  local copies, waits for them, and re-layouts  98.8 us (23%)
  starting transfers between devices  67.8 us (15%)
  matrix products  49.1 us (11%)
  other arithmetic  41.2 us (9%)
  blocking collectives  17.6 us (4%)
  between operations  14 us (3%)
    all_to_all x1, waiting for transfers between devices, per_device(): lax.all_to_all(full_input, 'context', split_axis=2, concat_axis=1, tiled=...  112 us
    unnamed x34, local copies, waits for them, and re-layouts  38.1 us
    unnamed x4, other arithmetic  29.2 us
    dot_general x12, matrix products, block_grads(): jnp.einsum('ghqk,ghqd->gkd', dscores, query_blk, preferred_element_type=j...  19.8 us
    all_to_all x1, blocking collectives, per_device(): lax.all_to_all(quantized[None], 'dp', split_axis=2, concat_axis=0, tiled=...  17.6 us
    dot_general x12, matrix products, block_grads(): jnp.einsum('ghqd,gkd->ghqk', query_blk, key_blk, preferred_element_type=j...  15.7 us
    ppermute x2, starting transfers between devices, per_device(): lax.ppermute(going_up, 'tensor', [(d, (d + 1) % ways) for d in range(ways)])  13.2 us
    ppermute x2, local copies, waits for them, and re-layouts, per_device(): lax.ppermute(going_up, 'tensor', [(d, (d + 1) % ways) for d in range(ways)])  10.6 us
  transfers between devices with their start and end apart: 20, of which 7 were waited for; matrix products, arithmetic and copies ran while one was open for 31% of the time, Pallas kernels for 0%

profile of v1, /device:TPU:6, one launch (start us, length us, event | category | flops | bytes accessed | tf_op | source)
XLA Modules:
  0.0 436.4 jit_solution(14889591473694256830)
XLA Ops:
  6.5 7.9 %collective-permute-start = (bf16[1,512,1024]{2,1,0:T(8,128)(2,1)}, bf16[1,512,1024]{2,1,0:T(8,128)(2,1)}, u32[]{:S(2)}, u32[]{:S(2)}) collective-permute-start(bf16[1,512,1024]{2,1,0:T(8,128)(2,1)} %param.13), channel_id=1, source_target_pairs={{0,1},{1,2},{2,3},{3,0},{4,5},{5,6},{6,7},{7,4},{8,9},{9,10},{10,1... | collective-permute-start | bytes 3145736 | tf_op jit(solution)/shard_map/ppermute | solution.py:202
  14.4 1.9 collective-permute-start.1
  21.2 3.5 all-to-all-start.3
  28.9 3.3 all-to-all-done.3
  32.2 3.9 all-to-all-start.6
  36.3 3.9 copy.97
  47.5 7.2 %all-to-all-start.1 = ((bf16[16,4,4096]{2,1,0:T(4,128)(2,1)}), bf16[16,4,4096]{2,1,0:T(4,128)(2,1)S(1)}, u32[]{:S(2)}, u32[]{:S(2)}) async-start(bf16[16,4,4096]{2,1,0:T(4,128)(2,1)} %copy.103), calls=%async_computation.1 | async-start | bytes 1048576 | tf_op jit(solution)/shard_map/all_to_all | solution.py:118
  55.7 5.5 %broadcast_in_dim.102 = bf16[1,512,4096]{1,0,2:T(2,128)(2,1)} broadcast(bf16[]{:T(256)} %constant.161.clone.1), dimensions={} | broadcast | bytes 4194306 | tf_op jit(solution)/shard_map/broadcast_in_dim | solution.py:198
  61.2 3.5 constant_dynamic-update-slice_fusion.3
  64.7 6.0 %all-to-all-done.1 = bf16[16,4,4096]{2,1,0:T(4,128)(2,1)S(1)} async-done(((bf16[16,4,4096]{2,1,0:T(4,128)(2,1)}), bf16[16,4,4096]{2,1,0:T(4,128)(2,1)S(1)}, u32[]{:S(2)}, u32[]{:S(2)}) %all-to-all-start.1) | async-done | bytes 524320 | tf_op jit(solution)/shard_map/all_to_all | solution.py:118
  70.7 4.2 all-to-all-start.4
  80.7 8.8 %collective-permute-done.6 = bf16[4,512]{1,0:T(4,128)(2,1)S(1)} collective-permute-done((bf16[4,512]{1,0:T(4,128)(2,1)S(1)}, bf16[4,512]{1,0:T(4,128)(2,1)S(1)}, u32[]{:S(2)}, u32[]{:S(2)}) %collective-permute-start.6) | collective-permute-done | bytes 4128 | tf_op jit(solution)/shard_map/ppermute | solution.py:17
  91.5 10.6 %all-to-all-start.2 = ((bf16[16,2,2048]{2,1,0:T(2,128)(2,1)}), bf16[16,2,2048]{2,1,0:T(2,128)(2,1)S(1)}, u32[]{:S(2)}, u32[]{:S(2)}) async-start(bf16[16,2,2048]{2,1,0:T(2,128)(2,1)} %reshape.395), calls=%async_computation.2 | async-start | bytes 262144 | tf_op jit(solution)/shard_map/all_to_all | solution.py:120
  104.1 6.7 %all-to-all-done.2 = bf16[16,2,2048]{2,1,0:T(2,128)(2,1)S(1)} async-done(((bf16[16,2,2048]{2,1,0:T(2,128)(2,1)}), bf16[16,2,2048]{2,1,0:T(2,128)(2,1)S(1)}, u32[]{:S(2)}, u32[]{:S(2)}) %all-to-all-start.2) | async-done | bytes 131104 | tf_op jit(solution)/shard_map/all_to_all | solution.py:120
  110.8 3.5 all-to-all-start.5
  117.5 5.6 %all-to-all-done.5 = bf16[16,2,2048]{2,1,0:T(2,128)(2,1)S(1)} async-done(((bf16[16,2,2048]{2,1,0:T(2,128)(2,1)}), bf16[16,2,2048]{2,1,0:T(2,128)(2,1)S(1)}, u32[]{:S(2)}, u32[]{:S(2)}) %all-to-all-start.5) | async-done | bytes 131104 | tf_op jit(solution)/shard_map/all_to_all | solution.py:121
  123.5 6.0 %copy.98 = bf16[1,512,1024]{1,0,2:T(2,128)(2,1)} copy(bf16[1,512,1024]{2,1,0:T(8,128)(2,1)} %collective-permute-done) | data formatting | bytes 2097152 | tf_op jit(solution)/shard_map/ppermute | solution.py:202
  129.5 5.3 %collective-permute-start.2 = (bf16[1,512,1024]{2,1,0:T(8,128)(2,1)}, bf16[1,512,1024]{2,1,0:T(8,128)(2,1)}, u32[]{:S(2)}, u32[]{:S(2)}) collective-permute-start(bf16[1,512,1024]{2,1,0:T(8,128)(2,1)} %collective-permute-done), channel_id=1, source_target_pairs={{0,1},{1,2},{2,3},{3,0},{4,5},{5,6},{6,7},{7,4},{8,9},{9,10},{10,1... | collective-permute-start | bytes 3145736 | tf_op jit(solution)/shard_map/ppermute | solution.py:202
  134.8 6.0 %copy.99 = bf16[1,512,1024]{1,0,2:T(2,128)(2,1)} copy(bf16[1,512,1024]{2,1,0:T(8,128)(2,1)} %collective-permute-done.1) | data formatting | bytes 2097152 | tf_op jit(solution)/shard_map/ppermute | solution.py:205
  140.8 2.3 pad_maximum_fusion
  144.5 44.4 %while.16 = (s32[]{:T(128)}, f32[1,512,128]{2,1,0:T(8,128)S(1)}, f32[1,512,128]{2,1,0:T(8,128)S(1)}, s32[1536]{0:T(1024)S(1)}, s32[512]{0:T(512)S(1)}, /*index=5...) while((s32[]{:T(128)}, f32[1,512,128]{2,1,0:T(8,128)S(1)}, ...), condition=%wide.region_7.8_spmd.clone, body=%wide.region_6.7_spmd.clone.sunk | while | flops 270796288 | bytes 5133037 | solution.py:180
  146.5 1.7 fusion.163
  150.2 1.7 fusion.163
  153.9 1.7 fusion.163
  157.6 1.7 fusion.163
  161.3 1.7 fusion.163
  165.0 1.7 fusion.163
  168.7 1.7 fusion.163
  172.4 1.7 fusion.163
  176.1 1.7 fusion.163
  179.8 1.7 fusion.163
  187.2 1.7 fusion.163
  191.5 4.5 %all-to-all-start.7 = ((bf16[16,2,4096]{2,1,0:T(2,128)(2,1)}), bf16[16,2,4096]{2,1,0:T(2,128)(2,1)S(1)}, u32[]{:S(2)}, u32[]{:S(2)}) async-start(bf16[16,2,4096]{2,1,0:T(2,128)(2,1)} %reshape.399), calls=%async_computation.7 | async-start | bytes 524288 | tf_op jit(solution)/shard_map/all_to_all | solution.py:190
  196.1 3.5 constant_dynamic-update-slice_fusion.2
  199.6 3.5 constant_dynamic-update-slice_fusion.1
  203.1 4.2 all-to-all-done.7
  207.5 4.6 %copy.100 = bf16[1,512,1024]{1,0,2:T(2,128)(2,1)S(1)} copy(bf16[1,512,1024]{2,1,0:T(8,128)(2,1)} %collective-permute-done.2) | data formatting | bytes 2097152 | tf_op jit(solution)/shard_map/ppermute | solution.py:202
  212.2 3.5 constant_dynamic-update-slice_fusion
  215.6 28.5 %reduce.7 = bf16[4096,512]{1,0:T(8,128)(2,1)} reduce(bf16[4096,1,512]{2,1,0:T(2,128)(2,1)} %bitcast.139, bf16[]{:T(256)} %broadcast.477), dimensions={1}, to_apply=%bitcast.139.reduce_sub_computation | reduce | bytes 8388610
  244.1 11.4 %reshape.393 = bf16[16,2,65536]{2,1,0:T(2,128)(2,1)} reshape(bf16[4096,512]{1,0:T(8,128)(2,1)} %reduce.7) | data formatting | bytes 8388608
  255.5 4.7 %all-to-all-start = ((bf16[16,2,65536]{2,1,0:T(2,128)(2,1)}), bf16[16,2,65536]{2,1,0:T(2,128)(2,1)}, u32[]{:S(2)}, u32[]{:S(2)}) async-start(bf16[16,2,65536]{2,1,0:T(2,128)(2,1)} %reshape.393), calls=%async_computation | async-start | bytes 8388608 | tf_op jit(solution)/shard_map/all_to_all | solution.py:212
  261.8 112.4 %all-to-all-done = bf16[16,2,65536]{2,1,0:T(2,128)(2,1)} async-done(((bf16[16,2,65536]{2,1,0:T(2,128)(2,1)}), bf16[16,2,65536]{2,1,0:T(2,128)(2,1)}, u32[]{:S(2)}, u32[]{:S(2)}) %all-to-all-start) | async-done | bytes 4194336 | tf_op jit(solution)/shard_map/all_to_all | solution.py:212
  374.1 12.4 %reshape.394 = bf16[4096,1,512]{2,1,0:T(2,128)(2,1)} reshape(bf16[16,2,65536]{2,1,0:T(2,128)(2,1)} %all-to-all-done) | data formatting | bytes 8388608
  386.5 6.5 %copy.121 = bf16[1,512,4096]{1,2,0:T(8,128)(2,1)} copy(bf16[1,512,4096]{1,0,2:T(2,128)(2,1)} %bitcast.161) | data formatting | bytes 8388608
  393.0 6.4 %copy.101 = bf16[1,16,512,256]{3,2,1,0:T(8,128)(2,1)} copy(bf16[1,16,512,256]{2,3,1,0:T(8,128)(2,1)} %bitcast.162) | data formatting | bytes 8388608 | tf_op jit(solution)/shard_map/all_to_all | solution.py:212
  399.5 6.3 %copy.102 = bf16[256,8192]{1,0:T(8,128)(2,1)} copy(bf16[256,8192]{0,1:T(8,128)(2,1)} %bitcast.163) | data formatting | bytes 8388608 | tf_op jit(solution)/shard_map/td,tc->dc/dot_general | solution.py:214
  405.8 4.7 %fusion.36 = f32[2,128,256]{2,1,0:T(8,128)S(1)} fusion(bf16[2,128,8192]{2,1,0:T(8,128)(2,1)} %bitcast.164, bf16[1,8192,256]{2,1,0:T(8,128)(2,1)} %all-gather.2.cloned.1.call-done, f32[2,128]{1,0:T(2,128)S(1)} %convert_element_type.175), kind=kOutput, calls=%fused_computation.53 | convolution fusion | flops 1073807360 | bytes 8651776 | tf_op jit(solution)/shard_map/td,tc->dc/dot_general | solution.py:214
  411.3 17.6 %all_to_all.66 = bf16[1,2,128,256]{3,1,0,2:T(2,128)(2,1)S(1)} all-to-all(bf16[1,2,128,256]{3,1,0,2:T(2,128)(2,1)S(1)} %copy.116), channel_id=1, replica_groups=mesh['dp'=8,'context'=16,'tensor'=4] {'dp'}, dimensions={2} | all-to-all | bytes 262144 | tf_op jit(solution)/shard_map/all_to_all | solution.py:229
  (208 shorter events, 63.0 us)
Async XLA Ops:
  6.5 29.8 %copy-start.3 = (bf16[1,512,1024]{2,1,0:T(8,128)(2,1)S(1)}, bf16[1,512,1024]{2,1,0:T(8,128)(2,1)}, u32[]{:S(2)}) copy-start(bf16[1,512,1024]{2,1,0:T(8,128)(2,1)} %param.13) | copy-start | bytes 3145732
  6.5 21.3 %copy-start.7 = (bf16[1,4,512]{2,1,0:T(4,128)(2,1)S(1)}, bf16[1,4,512]{2,1,0:T(4,128)(2,1)}, u32[]{:S(2)}) copy-start(bf16[1,4,512]{2,1,0:T(4,128)(2,1)} %param.19) | copy-start | bytes 12292
  6.5 21.5 %copy-start.4 = (bf16[1,1,512,128]{3,2,1,0:T(8,128)(2,1)S(1)}, bf16[1,1,512,128]{3,2,1,0:T(8,128)(2,1)}, u32[]{:S(2)}) copy-start(bf16[1,1,512,128]{3,2,1,0:T(8,128)(2,1)} %param.15) | copy-start | bytes 393220
  6.5 22.3 %copy-start.5 = (bf16[1,1,512,128]{3,2,1,0:T(8,128)(2,1)S(1)}, bf16[1,1,512,128]{3,2,1,0:T(8,128)(2,1)}, u32[]{:S(2)}) copy-start(bf16[1,1,512,128]{3,2,1,0:T(8,128)(2,1)} %param.16) | copy-start | bytes 393220
  6.5 109.1 %collective-permute-start = (bf16[1,512,1024]{2,1,0:T(8,128)(2,1)}, bf16[1,512,1024]{2,1,0:T(8,128)(2,1)}, u32[]{:S(2)}, u32[]{:S(2)}) collective-permute-start(bf16[1,512,1024]{2,1,0:T(8,128)(2,1)} %param.13), channel_id=1, source_target_pairs={{0,1},{1,2},{2,3},{3,0},{4,5},{5,6},{6,7},{7,4},{8,9},{9,10},{10,1... | collective-permute-start | bytes 3145736 | tf_op jit(solution)/shard_map/ppermute | solution.py:202
  14.4 115.1 %collective-permute-start.1 = (bf16[1,512,1024]{2,1,0:T(8,128)(2,1)}, bf16[1,512,1024]{2,1,0:T(8,128)(2,1)}, u32[]{:S(2)}, u32[]{:S(2)}) collective-permute-start(bf16[1,512,1024]{2,1,0:T(8,128)(2,1)} %param.13), channel_id=1, source_target_pairs={{0,3},{1,0},{2,1},{3,2},{4,7},{5,4},{6,5},{7,6},{8,11},{9,8},{10,9... | collective-permute-start | bytes 3145736 | tf_op jit(solution)/shard_map/ppermute | solution.py:205
  21.2 11.1 %all-to-all-start.3 = ((bf16[16,4,32]{2,1,0:T(4,128)(2,1)}), bf16[16,4,32]{2,1,0:T(4,128)(2,1)S(1)}, u32[]{:S(2)}, u32[]{:S(2)}) async-start(bf16[16,4,32]{2,1,0:T(4,128)(2,1)} %copy.106), calls=%async_computation.3 | async-start | bytes 32768 | tf_op jit(solution)/shard_map/all_to_all | solution.py:122
  27.5 14.5 %copy-start.6 = (s32[1,256]{1,0:T(1,128)S(1)}, s32[1,256]{1,0:T(1,128)}, u32[]{:S(2)}) copy-start(s32[1,256]{1,0:T(1,128)} %param.21) | copy-start | bytes 3076
  32.2 15.2 %all-to-all-start.6 = ((bf16[16,4,32]{2,1,0:T(4,128)(2,1)}), bf16[16,4,32]{2,1,0:T(4,128)(2,1)S(1)}, u32[]{:S(2)}, u32[]{:S(2)}) async-start(bf16[16,4,32]{2,1,0:T(4,128)(2,1)} %copy.111), calls=%async_computation.6 | async-start | bytes 32768 | tf_op jit(solution)/shard_map/all_to_all | solution.py:123
  36.3 11.0 %copy-start.9 = (s32[1,10]{1,0:T(1,128)S(1)}, s32[1,10]{1,0:T(1,128)}, u32[]{:S(2)}) copy-start(s32[1,10]{1,0:T(1,128)} %param.20) | copy-start | bytes 124
  47.5 23.3 %all-to-all-start.1 = ((bf16[16,4,4096]{2,1,0:T(4,128)(2,1)}), bf16[16,4,4096]{2,1,0:T(4,128)(2,1)S(1)}, u32[]{:S(2)}, u32[]{:S(2)}) async-start(bf16[16,4,4096]{2,1,0:T(4,128)(2,1)} %copy.103), calls=%async_computation.1 | async-start | bytes 1048576 | tf_op jit(solution)/shard_map/all_to_all | solution.py:118
  55.7 5.5 %copy-start.2 = (bf16[1,512,1024]{1,0,2:T(2,128)(2,1)S(1)}, bf16[1,512,1024]{1,0,2:T(2,128)(2,1)}, u32[]{:S(2)}) copy-start(bf16[1,512,1024]{1,0,2:T(2,128)(2,1)} %copy.97) | copy-start | bytes 3145732
  70.7 20.8 %all-to-all-start.4 = ((bf16[16,4,4096]{2,1,0:T(4,128)(2,1)}), bf16[16,4,4096]{2,1,0:T(4,128)(2,1)S(1)}, u32[]{:S(2)}, u32[]{:S(2)}) async-start(bf16[16,4,4096]{2,1,0:T(4,128)(2,1)} %copy.108), calls=%async_computation.4 | async-start | bytes 1048576 | tf_op jit(solution)/shard_map/all_to_all | solution.py:119
  75.2 4.2 collective-permute-start.5
  76.5 13.0 %collective-permute-start.6 = (bf16[4,512]{1,0:T(4,128)(2,1)S(1)}, bf16[4,512]{1,0:T(4,128)(2,1)S(1)}, u32[]{:S(2)}, u32[]{:S(2)}) collective-permute-start(bf16[4,512]{1,0:T(4,128)(2,1)S(1)} %squeeze_reshape.6), channel_id=1, source_target_pairs={{8,0},{12,4},{16,8},{20,12},{24,16},{28,20},{32,24},{36,28},{40,32... | collective-permute-start | bytes 12296 | tf_op jit(solution)/shard_map/ppermute | solution.py:17
  78.1 24.0 %collective-permute-start.10 = (bf16[4,512]{1,0:T(4,128)(2,1)S(1)}, bf16[4,512]{1,0:T(4,128)(2,1)S(1)}, u32[]{:S(2)}, u32[]{:S(2)}) collective-permute-start(bf16[4,512]{1,0:T(4,128)(2,1)S(1)} %squeeze_reshape.7), channel_id=1, source_target_pairs={{8,0},{12,4},{16,8},{20,12},{24,16},{28,20},{32,24},{36,28},{40,32... | collective-permute-start | bytes 12296 | tf_op jit(solution)/shard_map/ppermute | solution.py:17
  79.4 35.0 %collective-permute-start.9 = (bf16[4,512]{1,0:T(4,128)(2,1)S(1)}, bf16[4,512]{1,0:T(4,128)(2,1)S(1)}, u32[]{:S(2)}, u32[]{:S(2)}) collective-permute-start(bf16[4,512]{1,0:T(4,128)(2,1)S(1)} %squeeze_reshape.7), channel_id=1, source_target_pairs={{4,0},{8,4},{12,8},{16,12},{20,16},{24,20},{28,24},{32,28},{36,32}... | collective-permute-start | bytes 12296 | tf_op jit(solution)/shard_map/ppermute | solution.py:17
  90.2 50.6 %collective-permute-start.3 = (bf16[4,512,128]{2,1,0:T(8,128)(2,1)S(1)}, bf16[4,512,128]{2,1,0:T(8,128)(2,1)S(1)}, u32[]{:S(2)}, u32[]{:S(2)}) collective-permute-start(bf16[4,512,128]{2,1,0:T(8,128)(2,1)S(1)} %reshape.357), channel_id=1, source_target_pairs={{4,0},{8,4},{12,8},{16,12},{20,16},{24,20},{28,24},{32,28},{36,32}... | collective-permute-start | bytes 1572872 | tf_op jit(solution)/shard_map/ppermute | solution.py:17
  91.5 19.3 %all-to-all-start.2 = ((bf16[16,2,2048]{2,1,0:T(2,128)(2,1)}), bf16[16,2,2048]{2,1,0:T(2,128)(2,1)S(1)}, u32[]{:S(2)}, u32[]{:S(2)}) async-start(bf16[16,2,2048]{2,1,0:T(2,128)(2,1)} %reshape.395), calls=%async_computation.2 | async-start | bytes 262144 | tf_op jit(solution)/shard_map/all_to_all | solution.py:120
  102.1 38.7 %collective-permute-start.4 = (bf16[4,512,128]{2,1,0:T(8,128)(2,1)S(1)}, bf16[4,512,128]{2,1,0:T(8,128)(2,1)}, u32[]{:S(2)}, u32[]{:S(2)}) collective-permute-start(bf16[4,512,128]{2,1,0:T(8,128)(2,1)S(1)} %reshape.357), channel_id=1, source_target_pairs={{8,0},{12,4},{16,8},{20,12},{24,16},{28,20},{32,24},{36,28},{40,32... | collective-permute-start | bytes 1572872 | tf_op jit(solution)/shard_map/ppermute | solution.py:17
  110.8 12.2 %all-to-all-start.5 = ((bf16[16,2,2048]{2,1,0:T(2,128)(2,1)}), bf16[16,2,2048]{2,1,0:T(2,128)(2,1)S(1)}, u32[]{:S(2)}, u32[]{:S(2)}) async-start(bf16[16,2,2048]{2,1,0:T(2,128)(2,1)} %reshape.397), calls=%async_computation.5 | async-start | bytes 262144 | tf_op jit(solution)/shard_map/all_to_all | solution.py:121
  114.4 28.8 %collective-permute-start.7 = (bf16[4,512,128]{2,1,0:T(8,128)(2,1)S(1)}, bf16[4,512,128]{2,1,0:T(8,128)(2,1)}, u32[]{:S(2)}, u32[]{:S(2)}) collective-permute-start(bf16[4,512,128]{2,1,0:T(8,128)(2,1)S(1)} %reshape.361), channel_id=1, source_target_pairs={{4,0},{8,4},{12,8},{16,12},{20,16},{24,20},{28,24},{32,28},{36,32}... | collective-permute-start | bytes 1572872 | tf_op jit(solution)/shard_map/ppermute | solution.py:17
  115.7 27.5 %collective-permute-start.8 = (bf16[4,512,128]{2,1,0:T(8,128)(2,1)S(1)}, bf16[4,512,128]{2,1,0:T(8,128)(2,1)}, u32[]{:S(2)}, u32[]{:S(2)}) collective-permute-start(bf16[4,512,128]{2,1,0:T(8,128)(2,1)S(1)} %reshape.361), channel_id=1, source_target_pairs={{8,0},{12,4},{16,8},{20,12},{24,16},{28,20},{32,24},{36,28},{40,32... | collective-permute-start | bytes 1572872 | tf_op jit(solution)/shard_map/ppermute | solution.py:17
  129.5 78.0 %collective-permute-start.2 = (bf16[1,512,1024]{2,1,0:T(8,128)(2,1)}, bf16[1,512,1024]{2,1,0:T(8,128)(2,1)}, u32[]{:S(2)}, u32[]{:S(2)}) collective-permute-start(bf16[1,512,1024]{2,1,0:T(8,128)(2,1)} %collective-permute-done), channel_id=1, source_target_pairs={{0,1},{1,2},{2,3},{3,0},{4,5},{5,6},{6,7},{7,4},{8,9},{9,10},{10,1... | collective-permute-start | bytes 3145736 | tf_op jit(solution)/shard_map/ppermute | solution.py:202
  188.9 7.1 %copy-start = (bf16[1,512,1024]{1,0,2:T(2,128)(2,1)S(1)}, bf16[1,512,1024]{1,0,2:T(2,128)(2,1)}, u32[]{:S(2)}) copy-start(bf16[1,512,1024]{1,0,2:T(2,128)(2,1)} %copy.98) | copy-start | bytes 3145732
  191.5 15.7 %all-to-all-start.7 = ((bf16[16,2,4096]{2,1,0:T(2,128)(2,1)}), bf16[16,2,4096]{2,1,0:T(2,128)(2,1)S(1)}, u32[]{:S(2)}, u32[]{:S(2)}) async-start(bf16[16,2,4096]{2,1,0:T(2,128)(2,1)} %reshape.399), calls=%async_computation.7 | async-start | bytes 524288 | tf_op jit(solution)/shard_map/all_to_all | solution.py:190
  196.1 3.5 copy-start.1
  255.5 6.2 %copy-start.8 = (s32[2,128]{1,0:T(2,128)S(1)}, s32[2,128]{1,0:T(2,128)}, u32[]{:S(2)}) copy-start(s32[2,128]{1,0:T(2,128)} %param.22) | copy-start | bytes 3076
  255.5 6.2 %copy-start.10 = (s32[1,2]{1,0:T(1,128)S(1)}, s32[1,2]{1,0:T(1,128)}, u32[]{:S(2)}) copy-start(s32[1,2]{1,0:T(1,128)} %param.23) | copy-start | bytes 28
  255.5 118.6 %all-to-all-start = ((bf16[16,2,65536]{2,1,0:T(2,128)(2,1)}), bf16[16,2,65536]{2,1,0:T(2,128)(2,1)}, u32[]{:S(2)}, u32[]{:S(2)}) async-start(bf16[16,2,65536]{2,1,0:T(2,128)(2,1)} %reshape.393), calls=%async_computation | async-start | bytes 8388608 | tf_op jit(solution)/shard_map/all_to_all | solution.py:212
  260.2 145.6 %all-gather.2.cloned.1.call-start = ((), (), s32[]{:S(2)}) async-start(), calls=%async_computation.9 | async-start | bytes 4456448 | tf_op jit(solution)/shard_map/all_gather | solution.py:217
Sparse Core Ops, SparseCore 0:
  263.2 108.9 all-gather.1
